TPU v7x, 32 devices: a whole 2x2x4 slice. The times are simulated.
32 devices in a mesh: ctx: 32 (over z, y, x, core).
Axes of the slice: x: 2, y: 2, z: 4, core: 2. Of those that a mesh axis runs over, the one named last changes fastest.
Arguments:
- queries: bfloat16 [4096, 32, 128], P('ctx'), may hold values from -40 to 40
- keys: bfloat16 [4096, 32, 128], P('ctx'), may hold values from -40 to 40
- values: bfloat16 [4096, 32, 128], P('ctx'), may hold values from -6 to 6
- cu_seqlens: int32 [17], replicated, may hold values from 0 to 4096, as said below
- positions: int32 [4096], P('ctx'), may hold values from 0 to 511, as said below
Outputs:
- attended: bfloat16 [4096, 32, 128], P('ctx')
Inputs may be any that keep to these rules, and one draw needn't show every extreme that they name: `cu_seqlens`: document starts in increasing order followed by 4096; the first start is 0, every document holds at least one token, exactly one document holds 512 tokens and every other fewer. `positions`: each token's offset from the start of its document as given by cu_seqlens.
All inputs are finite; a program needn't handle non-finite values.
Results may differ from a plain program's by a relative error of at most 0.0059.
Values may be sent and summed in bfloat16 or wider, within the bound.
No kernel may reach another device: no remote copies, remote signals or barrier semaphores. Data moves between devices by JAX's collectives and lax.ppermute only.
A program may use at most 192 MiB of HBM per device.

v0:
```python
import jax
import jax.numpy as jnp
from jax import lax
from jax.sharding import PartitionSpec as P

rope_base = 500000.0
query_blocks = 16


def rotate(inputs, places):
    half_width = inputs.shape[-1] // 2
    ladder = jnp.arange(half_width, dtype=jnp.float32) * (2.0 / inputs.shape[-1])
    frequency = jnp.power(jnp.float32(rope_base), -ladder)
    angles = places.astype(jnp.float32)[:, None] * frequency[None, :]
    cosine = jnp.expand_dims(jnp.cos(angles), tuple(range(1, inputs.ndim - 1)))
    sine_part = jnp.expand_dims(jnp.sin(angles), tuple(range(1, inputs.ndim - 1)))
    widened = inputs.astype(jnp.float32)
    first_half = widened[..., :half_width]
    second_half = widened[..., half_width:]
    turned = jnp.concatenate(
        [
            first_half * cosine - second_half * sine_part,
            second_half * cosine + first_half * sine_part,
        ],
        axis=-1,
    )
    return turned.astype(jnp.bfloat16)


def document_ids(cu_seqlens, all_tokens):
    offsets = jnp.arange(all_tokens, dtype=jnp.int32)
    counted = jnp.sum((cu_seqlens[None, :] <= offsets[:, None]).astype(jnp.int32), axis=1)
    return counted - 1


def attend(head_q, head_k, head_v, owners):
    all_tokens, heads_here, head_width = head_q.shape
    logit_scale = head_width ** (-0.5)
    rows = all_tokens // query_blocks
    reach = all_tokens // 8
    pieces = []
    for block in range(query_blocks):
        first = block * rows
        stop = first + rows
        lowest = max(0, first - reach + 1)
        query_at = jnp.arange(first, stop, dtype=jnp.int32)
        key_at = jnp.arange(lowest, stop, dtype=jnp.int32)
        allowed = (
            (query_at[:, None] >= key_at[None, :])
            & (owners[first:stop, None] == owners[None, lowest:stop])
        )[None]
        attention_logits = (
            jnp.einsum(
                "qhd,khd->hqk",
                head_q[first:stop],
                head_k[lowest:stop],
                preferred_element_type=jnp.float32,
            )
            * logit_scale
        )
        row_top = jnp.max(jnp.where(allowed, attention_logits, -1e30), axis=-1, keepdims=True)
        weights = jnp.where(allowed, jnp.exp(attention_logits - row_top), 0.0)
        softmax_denominator = jnp.sum(weights, axis=-1)
        attention_result = jnp.einsum(
            "hqk,khd->qhd",
            weights.astype(jnp.bfloat16),
            head_v[lowest:stop],
            preferred_element_type=jnp.float32,
        )
        pieces.append(
            (attention_result / jnp.transpose(softmax_denominator)[:, :, None]).astype(jnp.bfloat16)
        )
    return jnp.concatenate(pieces, axis=0)


def on_device(queries, keys, values, cu_seqlens, positions):
    devices = lax.axis_size("ctx")
    local_tokens, head_count, head_width = queries.shape
    all_tokens = local_tokens * devices
    owners = document_ids(cu_seqlens, all_tokens)
    queries = rotate(queries, positions)
    keys = rotate(keys, positions)
    heads_here = head_count // devices

    def split(array):
        return array.reshape(local_tokens, devices, heads_here, head_width)

    head_q = lax.all_to_all(split(queries), "ctx", split_axis=1, concat_axis=0, tiled=True)
    head_k = lax.all_to_all(split(keys), "ctx", split_axis=1, concat_axis=0, tiled=True)
    head_v = lax.all_to_all(split(values), "ctx", split_axis=1, concat_axis=0, tiled=True)
    item_count = head_q.shape[2]
    head_q = head_q.reshape(all_tokens, item_count, head_width)
    head_k = head_k.reshape(all_tokens, item_count, head_width)
    head_v = head_v.reshape(all_tokens, item_count, head_width)
    mixed_here = attend(head_q, head_k, head_v, owners)
    attention_result = mixed_here.reshape(all_tokens, 1, item_count, head_width)
    returned = lax.all_to_all(attention_result, "ctx", split_axis=0, concat_axis=1, tiled=True)
    return returned.reshape(local_tokens, head_count, head_width)


def solution(mesh):
    return jax.shard_map(
        on_device,
        mesh=mesh,
        in_specs=(P("ctx", None, None), P("ctx", None, None), P("ctx", None, None), P(), P("ctx")),
        out_specs=P("ctx", None, None),
        check_vma=False,
    )
```

profile of v0, /device:TPU:9, one launch (start us, length us, event | category | flops | bytes accessed | tf_op | source)
XLA Modules:
  0.0 159.9 jit_solution(15001568550939170115)
XLA Ops:
  0.0 2.7 %copy.36 = bf16[128,32,128]{2,0,1:T(8,128)(2,1)} copy(bf16[128,32,128]{2,1,0:T(8,128)(2,1)} %param.7) | data formatting | bytes 2097152 | tf_op args[2]
  2.7 6.3 %all-to-all-start.2 = ((bf16[128,32,1,128]{3,0,2,1:T(8,128)(2,1)}), bf16[128,32,1,128]{3,0,2,1:T(8,128)(2,1)S(1)}, u32[]{:S(2)}, u32[]{:S(2)}) async-start(bf16[128,32,1,128]{3,0,2,1:T(8,128)(2,1)} %bitcast.441), calls=%async_computation.2 | async-start | bytes 2097152 | tf_op jit(solution)/shard_map/all_to_all | solution.py:90
  10.6 1.4 fusion.66
  12.0 1.6 %maximum_bitcast_fusion = bf16[128,32,1,128]{3,0,2,1:T(8,128)(2,1)} fusion(bf16[128,32,1,64]{3,0,1,2:T(8,128)(2,1)S(1)} %get-tuple-element.6, bf16[128,32,1,64]{3,0,1,2:T(8,128)(2,1)S(1)} %get-tuple-element.5), kind=kLoop, calls=%fused_computation.105 | loop fusion | flops 2097152 | bytes 2097152 | tf_op jit(solution)/shard_map/concatenate | solution.py:20
  13.6 20.7 %all-to-all-done.2 = bf16[128,32,1,128]{3,0,2,1:T(8,128)(2,1)S(1)} async-done(((bf16[128,32,1,128]{3,0,2,1:T(8,128)(2,1)}), bf16[128,32,1,128]{3,0,2,1:T(8,128)(2,1)S(1)}, u32[]{:S(2)}, u32[]{:S(2)}) %all-to-all-start.2) | async-done | bytes 1048608 | tf_op jit(solution)/shard_map/all_to_all | solution.py:90
  34.3 4.6 %all-to-all-start.1 = ((bf16[128,32,1,128]{3,0,2,1:T(8,128)(2,1)}), bf16[128,32,1,128]{3,0,2,1:T(8,128)(2,1)}, u32[]{:S(2)}, u32[]{:S(2)}) async-start(bf16[128,32,1,128]{3,0,2,1:T(8,128)(2,1)} %maximum_bitcast_fusion), calls=%async_computation.1 | async-start | bytes 2097152 | tf_op jit(solution)/shard_map/all_to_all | solution.py:89
  39.2 1.6 pad_maximum_fusion
  40.8 23.5 %all-to-all-done.1 = bf16[128,32,1,128]{3,0,2,1:T(8,128)(2,1)} async-done(((bf16[128,32,1,128]{3,0,2,1:T(8,128)(2,1)}), bf16[128,32,1,128]{3,0,2,1:T(8,128)(2,1)}, u32[]{:S(2)}, u32[]{:S(2)}) %all-to-all-start.1) | async-done | bytes 1048608 | tf_op jit(solution)/shard_map/all_to_all | solution.py:89
  64.3 4.7 %all-to-all-start = ((bf16[128,32,1,128]{3,0,2,1:T(8,128)(2,1)}), bf16[128,32,1,128]{3,0,2,1:T(8,128)(2,1)S(1)}, u32[]{:S(2)}, u32[]{:S(2)}) async-start(bf16[128,32,1,128]{3,0,2,1:T(8,128)(2,1)} %pad_maximum_fusion), calls=%async_computation | async-start | bytes 2097152 | tf_op jit(solution)/shard_map/all_to_all | solution.py:88
  75.7 18.4 %all-to-all-done = bf16[128,32,1,128]{3,0,2,1:T(8,128)(2,1)S(1)} async-done(((bf16[128,32,1,128]{3,0,2,1:T(8,128)(2,1)}), bf16[128,32,1,128]{3,0,2,1:T(8,128)(2,1)S(1)}, u32[]{:S(2)}, u32[]{:S(2)}) %all-to-all-start) | async-done | bytes 1048608 | tf_op jit(solution)/shard_map/all_to_all | solution.py:88
  97.2 1.3 select_reduce_fusion.12
  100.0 1.3 select_reduce_fusion.11
  104.2 1.3 select_reduce_fusion.9
  105.5 1.3 select_reduce_fusion.8
  108.4 1.3 select_reduce_fusion.7
  112.5 1.3 select_reduce_fusion.5
  113.8 1.3 select_reduce_fusion.4
  116.7 1.3 select_reduce_fusion.3
  118.0 1.3 select_reduce_fusion.2
  121.0 1.3 select_reduce_fusion.1
  122.4 1.3 select_reduce_fusion
  125.7 1.4 reduce.64
  127.4 29.6 %all_to_all.60 = bf16[32,2,8192]{2,1,0:T(2,128)(2,1)S(1)} all-to-all(bf16[32,2,8192]{2,1,0:T(2,128)(2,1)S(1)} %reshape.841), channel_id=1, replica_groups=mesh['ctx'=32] {'ctx'}, dimensions={0} | all-to-all | bytes 2097152 | tf_op jit(solution)/shard_map/all_to_all | solution.py:97
  158.2 1.6 %copy.31 = bf16[128,32,128]{2,1,0:T(8,128)(2,1)} copy(bf16[128,32,128]{2,0,1:T(8,128)(2,1)S(1)} %bitcast.442) | data formatting | bytes 2097152 | tf_op jit(solution)/shard_map/reshape | solution.py:98
  (102 shorter events, 26.6 us)
Async XLA Ops:
  0.0 9.0 %copy-start.11 = (s32[128]{0:T(128)S(1)}, s32[128]{0:T(128)}, u32[]{:S(2)}) copy-start(s32[128]{0:T(128)} %param.9) | copy-start | bytes 1540
  0.0 9.4 %copy-start = (bf16[128,32,128]{2,1,0:T(8,128)(2,1)S(1)}, bf16[128,32,128]{2,1,0:T(8,128)(2,1)}, u32[]{:S(2)}) copy-start(bf16[128,32,128]{2,1,0:T(8,128)(2,1)} %param.6) | copy-start | bytes 3145732
  2.7 31.6 %all-to-all-start.2 = ((bf16[128,32,1,128]{3,0,2,1:T(8,128)(2,1)}), bf16[128,32,1,128]{3,0,2,1:T(8,128)(2,1)S(1)}, u32[]{:S(2)}, u32[]{:S(2)}) async-start(bf16[128,32,1,128]{3,0,2,1:T(8,128)(2,1)} %bitcast.441), calls=%async_computation.2 | async-start | bytes 2097152 | tf_op jit(solution)/shard_map/all_to_all | solution.py:90
  9.0 1.2 copy-start.1
  12.0 27.1 %copy-start.10 = (s32[17]{0:T(128)S(1)}, s32[17]{0:T(128)}, u32[]{:S(2)}) copy-start(s32[17]{0:T(128)} %param.8) | copy-start | bytes 208
  34.3 29.9 %all-to-all-start.1 = ((bf16[128,32,1,128]{3,0,2,1:T(8,128)(2,1)}), bf16[128,32,1,128]{3,0,2,1:T(8,128)(2,1)}, u32[]{:S(2)}, u32[]{:S(2)}) async-start(bf16[128,32,1,128]{3,0,2,1:T(8,128)(2,1)} %maximum_bitcast_fusion), calls=%async_computation.1 | async-start | bytes 2097152 | tf_op jit(solution)/shard_map/all_to_all | solution.py:89
  64.3 29.8 %all-to-all-start = ((bf16[128,32,1,128]{3,0,2,1:T(8,128)(2,1)}), bf16[128,32,1,128]{3,0,2,1:T(8,128)(2,1)S(1)}, u32[]{:S(2)}, u32[]{:S(2)}) async-start(bf16[128,32,1,128]{3,0,2,1:T(8,128)(2,1)} %pad_maximum_fusion), calls=%async_computation | async-start | bytes 2097152 | tf_op jit(solution)/shard_map/all_to_all | solution.py:88
  94.5 1.3 copy-start.9
  95.2 2.0 %copy-start.8 = (s32[767]{0:T(1024)S(1)}, s32[767]{0:T(1024)}, u32[]{:S(2)}) copy-start(s32[767]{0:T(1024)} %iota_add_fusion.12) | copy-start | bytes 9208
  99.1 0.9 copy-start.7
  99.5 1.8 %copy-start.6 = (s32[767]{0:T(1024)S(1)}, s32[767]{0:T(1024)}, u32[]{:S(2)}) copy-start(s32[767]{0:T(1024)} %iota_add_fusion.10) | copy-start | bytes 9208
  103.3 0.9 copy-start.5
  103.7 1.8 %copy-start.4 = (s32[767]{0:T(1024)S(1)}, s32[767]{0:T(1024)}, u32[]{:S(2)}) copy-start(s32[767]{0:T(1024)} %iota_add_fusion.8) | copy-start | bytes 9208
  107.5 0.9 copy-start.3
  107.9 1.8 %copy-start.2 = (s32[767]{0:T(1024)S(1)}, s32[767]{0:T(1024)}, u32[]{:S(2)}) copy-start(s32[767]{0:T(1024)} %iota_add_fusion.6) | copy-start | bytes 9208
where the time goes:
time: 163 us; the launch traced here: 160 us
  waiting for transfers between devices  62.6 us (38%)
  blocking collectives  29.6 us (18%)
  matrix products  26 us (16%)
  other arithmetic  16.8 us (10%)
  starting transfers between devices  15.6 us (10%)
  local copies, waits for them, and re-layouts  8.82 us (5%)
    all_to_all x1, blocking collectives, on_device(): lax.all_to_all(attention_result, 'ctx', split_axis=0, concat_axis=1, tile...  29.6 us
    all_to_all x1, waiting for transfers between devices, on_device(): lax.all_to_all(split(keys), 'ctx', split_axis=1, concat_axis=0, tiled=True)  23.5 us
    all_to_all x1, waiting for transfers between devices, on_device(): lax.all_to_all(split(values), 'ctx', split_axis=1, concat_axis=0, tiled=T...  20.7 us
    dot_general x16, matrix products, attend(): jnp.einsum('qhd,khd->hqk', head_q[first:stop], head_k[lowest:stop], prefe...  19.2 us
    all_to_all x1, waiting for transfers between devices, on_device(): lax.all_to_all(split(queries), 'ctx', split_axis=1, concat_axis=0, tiled=...  18.4 us
    dot_general x16, matrix products, attend(): jnp.einsum('hqk,khd->qhd', weights.astype(jnp.bfloat16), head_v[lowest:st...  6.78 us
    all_to_all x1, starting transfers between devices, on_device(): lax.all_to_all(split(values), 'ctx', split_axis=1, concat_axis=0, tiled=T...  6.32 us
    reduce_sum x9, other arithmetic, attend(): softmax_denominator = jnp.sum(weights, axis=-1)  4.84 us
  transfers between devices with their start and end apart: 3, of which 3 were waited for; matrix products, arithmetic and copies ran while one was open for 8% of the time, Pallas kernels for 0%

commit v1 on v0

v1 whole, which is shorter than its diff:
```python
import functools

import jax
import jax.numpy as jnp
import numpy as np
from jax import lax
from jax.experimental import pallas as pl
from jax.experimental.pallas import tpu as pltpu
from jax.sharding import PartitionSpec as P

rope_base = 500000.0
head_pieces = 2
masked = -1e30

ANY = pl.BlockSpec(memory_space=pl.ANY)
VMEM = pl.BlockSpec(memory_space=pltpu.VMEM)
SMEM = pl.BlockSpec(memory_space=pltpu.SMEM)


def turn_tables(positions, width):
    half = width // 2
    ladder = jnp.arange(half, dtype=jnp.float32) * (2.0 / width)
    frequency = jnp.power(jnp.float32(rope_base), -ladder)
    angles = positions.astype(jnp.float32)[:, None] * frequency[None, :]
    cosine, sine = jnp.cos(angles), jnp.sin(angles)
    return jnp.concatenate([cosine, cosine], axis=1), jnp.concatenate([-sine, sine], axis=1)


def spread_kernel(turned, group, pieces, member, cosine, sine, *refs):
    inputs = refs[: len(turned)]
    rows = refs[-1]
    outs = refs[len(turned) : -1]
    tokens, _, width = inputs[0].shape
    heads = rows.shape[0] // tokens
    me = member[0]
    at = 0
    for peer in range(group):
        first = pl.multiple_of((me ^ peer) * heads, heads)
        parts = pieces[peer]
        for source in range(len(turned)):
            rows[...] = inputs[source][:, pl.ds(first, heads), :].astype(jnp.float32).reshape(tokens * heads, width)
            for head in range(heads):
                taken = rows[pl.ds(head, tokens, stride=heads), :]
                if turned[source]:
                    taken = taken * cosine[...] + pltpu.roll(taken, width // 2, 1) * sine[...]
                count = heads // parts
                out = outs[at + head // count]
                place = (source, head % count) if len(turned) > 1 else (head % count,)
                out[place] = taken.astype(jnp.bfloat16)
        at += parts


def spread(arrays, turned, group, pieces, member, cosine, sine):
    tokens, all_heads, width = arrays[0].shape
    heads = all_heads // group
    lead = (len(arrays),) if len(arrays) > 1 else ()
    shapes = []
    for peer in range(group):
        for _ in range(pieces[peer]):
            shapes.append(jax.ShapeDtypeStruct(lead + (heads // pieces[peer], tokens, width), jnp.bfloat16))
    outs = pl.pallas_call(
        functools.partial(spread_kernel, turned, group, pieces),
        out_shape=shapes,
        in_specs=[SMEM, VMEM, VMEM] + [VMEM] * len(arrays),
        out_specs=[VMEM] * len(shapes),
        scratch_shapes=[pltpu.VMEM((tokens * heads, width), jnp.float32)],
        name="spread",
    )(member, cosine, sine, *arrays)
    split, at = [], 0
    for peer in range(group):
        split.append(outs[at : at + pieces[peer]])
        at += pieces[peer]
    return split


def attend_kernel(group, heads, offsets, member, cu, *refs):
    early, own, asked = refs[:group], refs[group : 2 * group], refs[2 * group : 3 * group]
    outs = refs[3 * group : 4 * group]
    held, wanted, bias, result, head_sem, asked_sem, out_sem = refs[4 * group :]
    tokens, width = asked[0].shape[-2:]
    span = (group + 1) * tokens
    me = member[0]
    seat = me % group
    base = (me // group - 1) * (group * tokens)
    spots = cu.shape[0]

    for peer in range(group):
        pltpu.make_async_copy(
            asked[peer].at[pl.ds(offsets[2], heads)], wanted.at[seat ^ peer], asked_sem.at[peer]
        ).start()
    for head in range(heads):
        for peer in range(group):
            for side, (source, offset) in enumerate(((early[peer], offsets[0][peer]), (own[peer], offsets[1][peer]))):
                slot = pl.multiple_of((side * group + (seat ^ peer)) * tokens, tokens)
                pltpu.make_async_copy(
                    source.at[:, offset + head], held.at[:, head, pl.ds(slot, tokens), :], head_sem.at[head]
                ).start()

    def start_of(token):
        def later(at, best):
            return jnp.where(cu[at] <= token, cu[at], best)

        return lax.fori_loop(1, spots, later, cu[0])

    needed = []
    for block in range(group):
        first = base + (group + block) * tokens
        token = first + lax.broadcasted_iota(jnp.int32, (tokens, tokens), 0)
        begin = jnp.zeros((tokens, tokens), jnp.int32) + cu[0]
        for spot in range(1, spots):
            begin = jnp.where(token >= cu[spot], cu[spot], begin)
        for part in range(group + 1):
            at = base + (block + part) * tokens + lax.broadcasted_iota(jnp.int32, (tokens, tokens), 1)
            bias[block, :, part * tokens : (part + 1) * tokens] = jnp.where((at >= begin) & (at <= token), 0.0, masked)
        needed.append((first - start_of(first) + tokens - 1) // tokens + 1)

    sizes = sorted({min(2, group + 1), min(3, group + 1), group + 1})
    rate = np.float32(width**-0.5 * np.log2(np.e))

    for peer in range(group):
        pltpu.make_async_copy(
            asked[peer].at[pl.ds(offsets[2], heads)], wanted.at[seat ^ peer], asked_sem.at[peer]
        ).wait()

    def one_head(head, carry):
        pltpu.make_async_copy(held.at[:, head], held.at[:, head], head_sem.at[head]).wait()
        for block in range(group):

            def window(size, block=block):
                low = (group + 1 - size) * tokens
                keys = held[0, head, block * tokens + low : block * tokens + span, :]
                values = held[1, head, block * tokens + low : block * tokens + span, :]
                scores = lax.dot_general(
                    wanted[block, head], keys, (((1,), (1,)), ((), ())), preferred_element_type=jnp.float32
                )
                scores = scores + bias[block, :, low:]
                peak = jnp.max(scores, axis=1, keepdims=True)
                weights = jnp.exp2((scores - peak) * rate)
                total = jnp.sum(weights, axis=1, keepdims=True)
                mixed = jnp.dot(weights.astype(jnp.bfloat16), values, preferred_element_type=jnp.float32)
                result[block, head] = (mixed / total).astype(jnp.bfloat16)

            for at, size in enumerate(sizes):
                fits = needed[block] <= size
                if at > 0:
                    fits = fits & (needed[block] > sizes[at - 1])
                pl.when(fits)(functools.partial(window, size))
        return carry

    lax.fori_loop(0, heads, one_head, 0)
    for peer in range(group):
        pltpu.make_async_copy(result.at[seat ^ peer], outs[peer], out_sem.at[peer]).start()
    for peer in range(group):
        pltpu.make_async_copy(result.at[seat ^ peer], outs[peer], out_sem.at[peer]).wait()


def attend(group, heads, offsets, member, cu, early, own, asked):
    tokens, width = asked[0].shape[-2:]
    return pl.pallas_call(
        functools.partial(attend_kernel, group, heads, offsets),
        out_shape=[jax.ShapeDtypeStruct((heads, tokens, width), jnp.bfloat16)] * group,
        in_specs=[SMEM, SMEM] + [ANY] * (3 * group),
        out_specs=[ANY] * group,
        scratch_shapes=[
            pltpu.VMEM((2, heads, 2 * group * tokens, width), jnp.bfloat16),
            pltpu.VMEM((group, heads, tokens, width), jnp.bfloat16),
            pltpu.VMEM((group, tokens, (group + 1) * tokens), jnp.float32),
            pltpu.VMEM((group, heads, tokens, width), jnp.bfloat16),
            pltpu.SemaphoreType.DMA((heads,)),
            pltpu.SemaphoreType.DMA((group,)),
            pltpu.SemaphoreType.DMA((group,)),
        ],
        name="attend",
    )(member, cu, *early, *own, *asked)


def gather_kernel(group, runs, member, *refs):
    rows, out = refs[-1], refs[-2]
    tokens, _, width = out.shape
    heads = rows.shape[0] // tokens
    count = heads // runs
    me = member[0]
    for peer in range(group):
        for head in range(heads):
            piece = refs[peer * runs + head // count]
            rows[pl.ds(head, tokens, stride=heads), :] = piece[head % count].astype(jnp.float32)
        first = pl.multiple_of((me ^ peer) * heads, heads)
        out[:, pl.ds(first, heads), :] = rows[...].reshape(tokens, heads, width).astype(jnp.bfloat16)


def gather(pieces, group, runs, member, shape):
    tokens, all_heads, width = shape
    return pl.pallas_call(
        functools.partial(gather_kernel, group, runs),
        out_shape=jax.ShapeDtypeStruct(shape, jnp.bfloat16),
        in_specs=[SMEM] + [VMEM] * len(pieces),
        out_specs=VMEM,
        scratch_shapes=[pltpu.VMEM((tokens * all_heads // group, width), jnp.float32)],
        name="gather",
    )(member, *pieces)


def on_device(queries, keys, values, cu_seqlens, positions):
    devices = lax.axis_size("ctx")
    tokens, all_heads, width = queries.shape
    reach = tokens * devices // 8
    group = reach // tokens
    heads = all_heads // group
    count = heads // head_pieces
    me = lax.axis_index("ctx").astype(jnp.int32)
    seat = (me % group)[None]
    me = me[None]
    swap = [[(device, device ^ peer) for device in range(devices)] for peer in range(group)]
    onward = [(device, device + group) for device in range(devices - group)]

    def send(array, pairs):
        return lax.ppermute(array, "ctx", pairs)

    pieces = tuple(1 if peer < 2 else head_pieces for peer in range(group))
    cosine, sine = turn_tables(positions, width)
    stored = spread((keys, values), (True, False), group, pieces, seat, cosine, sine)
    asked = spread((queries,), (True,), group, (1,) * group, seat, cosine, sine)

    own = [list(stored[peer]) for peer in range(group)]
    early = [[] for _ in range(group)]
    for peer in range(group):
        for piece in range(pieces[peer]):
            if peer > 0:
                own[peer][piece] = send(stored[peer][piece], swap[peer])
            early[peer].append(send(own[peer][piece], onward))
    asked = [asked[0][0]] + [send(asked[peer][0], swap[peer]) for peer in range(1, group)]

    back = [[] for _ in range(group)]
    for piece in range(head_pieces):
        starts = tuple(piece * count if pieces[peer] == 1 else 0 for peer in range(group))
        picked = [own[peer][0 if pieces[peer] == 1 else piece] for peer in range(group)]
        before = [early[peer][0 if pieces[peer] == 1 else piece] for peer in range(group)]
        mixed = attend(group, count, (starts, starts, piece * count), me, cu_seqlens, before, picked, asked)
        for peer in range(group):
            back[peer].append(mixed[peer] if peer == 0 else send(mixed[peer], swap[peer]))
    flat = [array for peer in range(group) for array in back[peer]]
    return gather(flat, group, head_pieces, seat, queries.shape)


def solution(mesh):
    return jax.shard_map(
        on_device,
        mesh=mesh,
        in_specs=(P("ctx", None, None), P("ctx", None, None), P("ctx", None, None), P(), P("ctx")),
        out_specs=P("ctx", None, None),
        check_vma=False,
    )
```

time: 163 us -> 98.8 us (0.61); the launches traced: 160 us -> 98.4 us
  Pallas kernels: 0 us -> 30.6 us
  waiting for transfers between devices: 62.6 us -> 32 us
  blocking collectives: 29.6 us -> 0 us
  matrix products: 26 us -> 0 us
  starting transfers between devices: 15.6 us -> 31.5 us
  other arithmetic: 16.8 us -> 1.08 us
  local copies, waits for them, and re-layouts: 8.82 us -> 3.06 us
    all_to_all x3 -> x0, waiting for transfers between devices: 62.6 us -> none  [the longest x1 23.5 us: on_device(): lax.all_to_all(split(keys), 'ctx', split_axis=1, concat_axis=0, tiled=True)]
    ppermute x0 -> x20, waiting for transfers between devices: none -> 32 us  [send(): return lax.ppermute(array, 'ctx', pairs)]
    ppermute x0 -> x20, starting transfers between devices: none -> 31.5 us  [send(): return lax.ppermute(array, 'ctx', pairs)]
    pallas_call x0 -> x5, Pallas kernels: none -> 30.6 us  [the longest x2 21.1 us: attend(): pl.pallas_call(functools.partial(attend_kernel, group, heads, offsets), o...]
    all_to_all x1 -> x0, blocking collectives: 29.6 us -> none  [on_device(): lax.all_to_all(attention_result, 'ctx', split_axis=0, concat_axis=1, tile...]
    dot_general x32 -> x0, matrix products: 26 us -> none  [the longest x16 19.2 us: attend(): jnp.einsum('qhd,khd->hqk', head_q[first:stop], head_k[lowest:stop], prefe...]
    all_to_all x3 -> x0, starting transfers between devices: 15.6 us -> none  [the longest x1 6.32 us: on_device(): lax.all_to_all(split(values), 'ctx', split_axis=1, concat_axis=0, tiled=T...]
    reduce_sum x10 -> x0, other arithmetic: 4.97 us -> none  [the longest x9 4.84 us: attend(): softmax_denominator = jnp.sum(weights, axis=-1)]
  transfers between devices with their start and end apart: 3 -> 20, of which waited for: 3 -> 9; matrix products, arithmetic and copies ran while one was open for 8% -> 0% of each run, Pallas kernels for 0% -> 24%
where the time goes in v1:
time: 98.8 us; the launch traced here: 98.4 us
  waiting for transfers between devices  32 us (32%)
  starting transfers between devices  31.5 us (32%)
  Pallas kernels  30.6 us (31%)
  local copies, waits for them, and re-layouts  3.06 us (3%)
  other arithmetic  1.08 us (1%)
    ppermute x20, waiting for transfers between devices, send(): return lax.ppermute(array, 'ctx', pairs)  32 us
    ppermute x20, starting transfers between devices, send(): return lax.ppermute(array, 'ctx', pairs)  31.5 us
    pallas_call x2, Pallas kernels, attend(): pl.pallas_call(functools.partial(attend_kernel, group, heads, offsets), o...  21.1 us
    pallas_call x2, Pallas kernels, spread(): pl.pallas_call(functools.partial(spread_kernel, turned, group, pieces), o...  6.69 us
    unnamed x38, local copies, waits for them, and re-layouts  3.06 us
    pallas_call x1, Pallas kernels, gather(): pl.pallas_call(functools.partial(gather_kernel, group, runs), out_shape=j...  2.84 us
  transfers between devices with their start and end apart: 20, of which 9 were waited for; matrix products, arithmetic and copies ran while one was open for 0% of the time, Pallas kernels for 24%

profile of v1, /device:TPU:9, one launch (start us, length us, event | category | flops | bytes accessed | tf_op | source)
XLA Modules:
  0.0 98.4 jit_solution(1108454413906356322)
XLA Ops:
  1.7 3.7 %spread.2 = (bf16[2,8,128,128]{3,2,1,0:T(8,128)(2,1)}, bf16[2,8,128,128]{3,2,1,0:T(8,128)(2,1)}, bf16[2,4,128,128]{3,2,1,0:T(8,128)(2,1)}, bf16[2,4,128,128]{3,2...) custom-call(s32[1]{0:T(128)} %bitcast.member, ...), custom_call_target="tpu_custom_call" | custom-call | tf_op jit(solution)/shard_map/spread/pallas_call | solution.py:61
  7.8 2.9 %spread.3 = (bf16[8,128,128]{2,1,0:T(8,128)(2,1)}, bf16[8,128,128]{2,1,0:T(8,128)(2,1)}, bf16[8,128,128]{2,1,0:T(8,128)(2,1)}, bf16[8,128,128]{2,1,0:T(8,128)(2,1)}) custom-call(s32[1]{0:T(128)} %bitcast.member, f32[128,128]{1,0:T(8,128)} %get-tuple-element.44.cosine, f32[128,128]{1,0:T(8,128)} %get-tuple-element.45.sine, bf16[128,32,128]{2,1,0:T(8,128)(2,1)} %refs_0_.3), custom_call_target="tpu_custom_call" | custom-call | tf_op jit(solution)/shard_map/spread/pallas_call | solution.py:61
  12.1 2.1 %collective-permute-done.10.refs_6_ = bf16[2,4,128,128]{3,2,1,0:T(8,128)(2,1)S(1)} collective-permute-done((bf16[2,4,128,128]{3,2,1,0:T(8,128)(2,1)}, bf16[2,4,128,128]{3,2,1,0:T(8,128)(2,1)S(1)}, u32[]{:S(2)}, u32[]{:S(2)}) %collective-permute-start.10) | collective-permute-done | bytes 262176 | tf_op jit(solution)/shard_map/ppermute | solution.py:217
  14.2 2.4 %collective-permute-start.9 = (bf16[8,128,128]{2,1,0:T(8,128)(2,1)}, bf16[8,128,128]{2,1,0:T(8,128)(2,1)S(1)}, u32[]{:S(2)}, u32[]{:S(2)}) collective-permute-start(bf16[8,128,128]{2,1,0:T(8,128)(2,1)} %get-tuple-element.30), channel_id=1, source_target_pairs={{0,3},{1,2},{2,1},{3,0},{4,7},{5,6},{6,5},{7,4},{8,11},{9,10},{10,... | collective-permute-start | bytes 786440 | tf_op jit(solution)/shard_map/ppermute | solution.py:217
  16.6 3.8 %collective-permute-done.12.refs_7_ = bf16[2,4,128,128]{3,2,1,0:T(8,128)(2,1)S(1)} collective-permute-done((bf16[2,4,128,128]{3,2,1,0:T(8,128)(2,1)}, bf16[2,4,128,128]{3,2,1,0:T(8,128)(2,1)S(1)}, u32[]{:S(2)}, u32[]{:S(2)}) %collective-permute-start.12) | collective-permute-done | bytes 262176 | tf_op jit(solution)/shard_map/ppermute | solution.py:217
  22.4 3.1 %collective-permute-start = (bf16[2,8,128,128]{3,2,1,0:T(8,128)(2,1)S(1)}, bf16[2,8,128,128]{3,2,1,0:T(8,128)(2,1)S(1)}, u32[]{:S(2)}, u32[]{:S(2)}) collective-permute-start(bf16[2,8,128,128]{3,2,1,0:T(8,128)(2,1)S(1)} %copy-done), channel_id=1, source_target_pairs={{0,4},{1,5},{2,6},{3,7},{4,8},{5,9},{6,10},{7,11},{8,12},{9,13},{1... | collective-permute-start | bytes 1572872 | tf_op jit(solution)/shard_map/ppermute | solution.py:217
  25.6 3.1 %collective-permute-start.2 = (bf16[2,8,128,128]{3,2,1,0:T(8,128)(2,1)S(1)}, bf16[2,8,128,128]{3,2,1,0:T(8,128)(2,1)S(1)}, u32[]{:S(2)}, u32[]{:S(2)}) collective-permute-start(bf16[2,8,128,128]{3,2,1,0:T(8,128)(2,1)S(1)} %collective-permute-done.1.refs_5_), channel_id=1, source_target_pairs={{0,4},{1,5},{2,6},{3,7},{4,8},{5,9},{6,10},{7,11},{8,12},{9,13},{1... | collective-permute-start | bytes 1572872 | tf_op jit(solution)/shard_map/ppermute | solution.py:217
  29.6 2.4 %collective-permute-done.9.refs_11_ = bf16[8,128,128]{2,1,0:T(8,128)(2,1)S(1)} collective-permute-done((bf16[8,128,128]{2,1,0:T(8,128)(2,1)}, bf16[8,128,128]{2,1,0:T(8,128)(2,1)S(1)}, u32[]{:S(2)}, u32[]{:S(2)}) %collective-permute-start.9) | collective-permute-done | bytes 262176 | tf_op jit(solution)/shard_map/ppermute | solution.py:217
  32.0 3.1 %collective-permute-start.11 = (bf16[2,4,128,128]{3,2,1,0:T(8,128)(2,1)S(1)}, bf16[2,4,128,128]{3,2,1,0:T(8,128)(2,1)S(1)}, u32[]{:S(2)}, u32[]{:S(2)}) collective-permute-start(bf16[2,4,128,128]{3,2,1,0:T(8,128)(2,1)S(1)} %collective-permute-done.10.refs_6_), channel_id=1, source_target_pairs={{0,4},{1,5},{2,6},{3,7},{4,8},{5,9},{6,10},{7,11},{8,12},{9,13},{1... | collective-permute-start | bytes 786440 | tf_op jit(solution)/shard_map/ppermute | solution.py:217
  35.2 1.5 %collective-permute-done.3.refs_6_ = bf16[2,4,128,128]{3,2,1,0:T(8,128)(2,1)S(1)} collective-permute-done((bf16[2,4,128,128]{3,2,1,0:T(8,128)(2,1)}, bf16[2,4,128,128]{3,2,1,0:T(8,128)(2,1)S(1)}, u32[]{:S(2)}, u32[]{:S(2)}) %collective-permute-start.3) | collective-permute-done | bytes 262176 | tf_op jit(solution)/shard_map/ppermute | solution.py:217
  36.7 3.1 %collective-permute-start.13 = (bf16[2,4,128,128]{3,2,1,0:T(8,128)(2,1)}, bf16[2,4,128,128]{3,2,1,0:T(8,128)(2,1)S(1)}, u32[]{:S(2)}, u32[]{:S(2)}) collective-permute-start(bf16[2,4,128,128]{3,2,1,0:T(8,128)(2,1)} %copy-done.9), channel_id=1, source_target_pairs={{0,4},{1,5},{2,6},{3,7},{4,8},{5,9},{6,10},{7,11},{8,12},{9,13},{1... | collective-permute-start | bytes 786440 | tf_op jit(solution)/shard_map/ppermute | solution.py:217
  39.8 2.9 %collective-permute-done.5.refs_7_ = bf16[2,4,128,128]{3,2,1,0:T(8,128)(2,1)} collective-permute-done((bf16[2,4,128,128]{3,2,1,0:T(8,128)(2,1)}, bf16[2,4,128,128]{3,2,1,0:T(8,128)(2,1)}, u32[]{:S(2)}, u32[]{:S(2)}) %collective-permute-start.5) | collective-permute-done | bytes 262176 | tf_op jit(solution)/shard_map/ppermute | solution.py:217
  42.8 3.1 %collective-permute-start.4 = (bf16[2,4,128,128]{3,2,1,0:T(8,128)(2,1)S(1)}, bf16[2,4,128,128]{3,2,1,0:T(8,128)(2,1)}, u32[]{:S(2)}, u32[]{:S(2)}) collective-permute-start(bf16[2,4,128,128]{3,2,1,0:T(8,128)(2,1)S(1)} %collective-permute-done.3.refs_6_), channel_id=1, source_target_pairs={{0,4},{1,5},{2,6},{3,7},{4,8},{5,9},{6,10},{7,11},{8,12},{9,13},{1... | collective-permute-start | bytes 786440 | tf_op jit(solution)/shard_map/ppermute | solution.py:217
  45.9 9.5 %collective-permute-done.11.refs_2_ = bf16[2,4,128,128]{3,2,1,0:T(8,128)(2,1)S(1)} collective-permute-done((bf16[2,4,128,128]{3,2,1,0:T(8,128)(2,1)S(1)}, bf16[2,4,128,128]{3,2,1,0:T(8,128)(2,1)S(1)}, u32[]{:S(2)}, u32[]{:S(2)}) %collective-permute-start.11) | collective-permute-done | bytes 262176 | tf_op jit(solution)/shard_map/ppermute | solution.py:217
  55.5 2.2 %collective-permute-start.6 = (bf16[2,4,128,128]{3,2,1,0:T(8,128)(2,1)}, bf16[2,4,128,128]{3,2,1,0:T(8,128)(2,1)}, u32[]{:S(2)}, u32[]{:S(2)}) collective-permute-start(bf16[2,4,128,128]{3,2,1,0:T(8,128)(2,1)} %collective-permute-done.5.refs_7_), channel_id=1, source_target_pairs={{0,4},{1,5},{2,6},{3,7},{4,8},{5,9},{6,10},{7,11},{8,12},{9,13},{1... | collective-permute-start | bytes 786440 | tf_op jit(solution)/shard_map/ppermute | solution.py:217
  57.7 3.4 %collective-permute-done.13.refs_3_ = bf16[2,4,128,128]{3,2,1,0:T(8,128)(2,1)S(1)} collective-permute-done((bf16[2,4,128,128]{3,2,1,0:T(8,128)(2,1)}, bf16[2,4,128,128]{3,2,1,0:T(8,128)(2,1)S(1)}, u32[]{:S(2)}, u32[]{:S(2)}) %collective-permute-start.13) | collective-permute-done | bytes 262176 | tf_op jit(solution)/shard_map/ppermute | solution.py:217
  62.2 10.5 %attend.3 = (bf16[4,128,128]{2,1,0:T(8,128)(2,1)}, bf16[4,128,128]{2,1,0:T(8,128)(2,1)}, bf16[4,128,128]{2,1,0:T(8,128)(2,1)}, bf16[4,128,128]{2,1,0:T(8,128)(2,1)}) custom-call(s32[1]{0:T(128)} %bitcast.1.member, s32[17]{0:T(128)} %cu.3, bf16[2,8,128,128]{3,2,1,0:T(8,128)(2,1)} %copy-done.2, bf16[2,8,128,128]{3,2,1,0:T(8,128)(2,1)} %copy-done.3, ...), custom_call_target="tpu_custom_call" | custom-call | tf_op jit(solution)/shard_map/attend/pallas_call | solution.py:159
  72.7 1.5 %collective-permute-start.15 = (bf16[4,128,128]{2,1,0:T(8,128)(2,1)}, bf16[4,128,128]{2,1,0:T(8,128)(2,1)S(1)}, u32[]{:S(2)}, u32[]{:S(2)}) collective-permute-start(bf16[4,128,128]{2,1,0:T(8,128)(2,1)} %get-tuple-element.36), channel_id=1, source_target_pairs={{0,1},{1,0},{2,3},{3,2},{4,5},{5,4},{6,7},{7,6},{8,9},{9,8},{10,11... | collective-permute-start | bytes 393224 | tf_op jit(solution)/shard_map/ppermute | solution.py:217
  74.5 1.4 %collective-permute-start.19 = (bf16[4,128,128]{2,1,0:T(8,128)(2,1)}, bf16[4,128,128]{2,1,0:T(8,128)(2,1)S(1)}, u32[]{:S(2)}, u32[]{:S(2)}) collective-permute-start(bf16[4,128,128]{2,1,0:T(8,128)(2,1)} %get-tuple-element.40), channel_id=1, source_target_pairs={{0,3},{1,2},{2,1},{3,0},{4,7},{5,6},{6,5},{7,4},{8,11},{9,10},{10,... | collective-permute-start | bytes 393224 | tf_op jit(solution)/shard_map/ppermute | solution.py:217
  75.9 10.5 %attend.2 = (bf16[4,128,128]{2,1,0:T(8,128)(2,1)}, bf16[4,128,128]{2,1,0:T(8,128)(2,1)}, bf16[4,128,128]{2,1,0:T(8,128)(2,1)}, bf16[4,128,128]{2,1,0:T(8,128)(2,1)}) custom-call(s32[1]{0:T(128)} %bitcast.1.member, s32[17]{0:T(128)} %cu.3, bf16[2,8,128,128]{3,2,1,0:T(8,128)(2,1)} %copy-done.2, bf16[2,8,128,128]{3,2,1,0:T(8,128)(2,1)} %copy-done.3, ...), custom_call_target="tpu_custom_call" | custom-call | tf_op jit(solution)/shard_map/attend/pallas_call | solution.py:159
  87.0 1.7 %collective-permute-start.18 = (bf16[4,128,128]{2,1,0:T(8,128)(2,1)}, bf16[4,128,128]{2,1,0:T(8,128)(2,1)S(1)}, u32[]{:S(2)}, u32[]{:S(2)}) collective-permute-start(bf16[4,128,128]{2,1,0:T(8,128)(2,1)} %get-tuple-element.39), channel_id=1, source_target_pairs={{0,3},{1,2},{2,1},{3,0},{4,7},{5,6},{6,5},{7,4},{8,11},{9,10},{10,... | collective-permute-start | bytes 393224 | tf_op jit(solution)/shard_map/ppermute | solution.py:217
  88.7 2.9 %collective-permute-done.16.refs_4_ = bf16[4,128,128]{2,1,0:T(8,128)(2,1)S(1)} collective-permute-done((bf16[4,128,128]{2,1,0:T(8,128)(2,1)}, bf16[4,128,128]{2,1,0:T(8,128)(2,1)S(1)}, u32[]{:S(2)}, u32[]{:S(2)}) %collective-permute-start.16) | collective-permute-done | bytes 131104 | tf_op jit(solution)/shard_map/ppermute | solution.py:217
  91.6 3.3 %collective-permute-done.18.refs_6_ = bf16[4,128,128]{2,1,0:T(8,128)(2,1)S(1)} collective-permute-done((bf16[4,128,128]{2,1,0:T(8,128)(2,1)}, bf16[4,128,128]{2,1,0:T(8,128)(2,1)S(1)}, u32[]{:S(2)}, u32[]{:S(2)}) %collective-permute-start.18) | collective-permute-done | bytes 131104 | tf_op jit(solution)/shard_map/ppermute | solution.py:217
  95.6 2.8 %gather.1 = bf16[128,32,128]{2,1,0:T(8,128)(2,1)} custom-call(s32[1]{0:T(128)} %bitcast.member, bf16[4,128,128]{2,1,0:T(8,128)(2,1)} %get-tuple-element.31.refs_0_, bf16[4,128,128]{2,1,0:T(8,128)(2,1)} %get-tuple-element.34.refs_1_, bf16[4,128,128]{2,1,0:T(8,128)(2,1)} %copy-done.15, bf16[4,128,128]{2,1,0:T(8,128)(2,1)} %copy-done.12, ...), custom_call_target="tpu_custom_call" | custom-call | tf_op jit(solution)/shard_map/gather/pallas_call | solution.py:193
  (63 shorter events, 10.7 us)
Async XLA Ops:
  5.5 20.1 %collective-permute-start.1 = (bf16[2,8,128,128]{3,2,1,0:T(8,128)(2,1)}, bf16[2,8,128,128]{3,2,1,0:T(8,128)(2,1)S(1)}, u32[]{:S(2)}, u32[]{:S(2)}) collective-permute-start(bf16[2,8,128,128]{3,2,1,0:T(8,128)(2,1)} %get-tuple-element.24), channel_id=1, source_target_pairs={{0,1},{1,0},{2,3},{3,2},{4,5},{5,4},{6,7},{7,6},{8,9},{9,8},{10,11... | collective-permute-start | bytes 1572872 | tf_op jit(solution)/shard_map/ppermute | solution.py:217
  6.2 8.1 %collective-permute-start.10 = (bf16[2,4,128,128]{3,2,1,0:T(8,128)(2,1)}, bf16[2,4,128,128]{3,2,1,0:T(8,128)(2,1)S(1)}, u32[]{:S(2)}, u32[]{:S(2)}) collective-permute-start(bf16[2,4,128,128]{3,2,1,0:T(8,128)(2,1)} %get-tuple-element.32), channel_id=1, source_target_pairs={{0,2},{1,3},{2,0},{3,1},{4,6},{5,7},{6,4},{7,5},{8,10},{9,11},{10,... | collective-permute-start | bytes 786440 | tf_op jit(solution)/shard_map/ppermute | solution.py:217
  7.4 13.1 %collective-permute-start.12 = (bf16[2,4,128,128]{3,2,1,0:T(8,128)(2,1)}, bf16[2,4,128,128]{3,2,1,0:T(8,128)(2,1)S(1)}, u32[]{:S(2)}, u32[]{:S(2)}) collective-permute-start(bf16[2,4,128,128]{3,2,1,0:T(8,128)(2,1)} %get-tuple-element.33), channel_id=1, source_target_pairs={{0,3},{1,2},{2,1},{3,0},{4,7},{5,6},{6,5},{7,4},{8,11},{9,10},{10,... | collective-permute-start | bytes 786440 | tf_op jit(solution)/shard_map/ppermute | solution.py:217
  10.7 11.7 %collective-permute-start.7 = (bf16[8,128,128]{2,1,0:T(8,128)(2,1)}, bf16[8,128,128]{2,1,0:T(8,128)(2,1)S(1)}, u32[]{:S(2)}, u32[]{:S(2)}) collective-permute-start(bf16[8,128,128]{2,1,0:T(8,128)(2,1)} %get-tuple-element.28), channel_id=1, source_target_pairs={{0,1},{1,0},{2,3},{3,2},{4,5},{5,4},{6,7},{7,6},{8,9},{9,8},{10,11... | collective-permute-start | bytes 786440 | tf_op jit(solution)/shard_map/ppermute | solution.py:217
  11.0 17.8 %collective-permute-start.8 = (bf16[8,128,128]{2,1,0:T(8,128)(2,1)}, bf16[8,128,128]{2,1,0:T(8,128)(2,1)S(1)}, u32[]{:S(2)}, u32[]{:S(2)}) collective-permute-start(bf16[8,128,128]{2,1,0:T(8,128)(2,1)} %get-tuple-element.29), channel_id=1, source_target_pairs={{0,2},{1,3},{2,0},{3,1},{4,6},{5,7},{6,4},{7,5},{8,10},{9,11},{10,... | collective-permute-start | bytes 786440 | tf_op jit(solution)/shard_map/ppermute | solution.py:217
  14.2 47.6 %copy-start.7 = (bf16[2,4,128,128]{3,2,1,0:T(8,128)(2,1)}, bf16[2,4,128,128]{3,2,1,0:T(8,128)(2,1)S(1)}, u32[]{:S(2)}) copy-start(bf16[2,4,128,128]{3,2,1,0:T(8,128)(2,1)S(1)} %collective-permute-done.10.refs_6_) | copy-start | bytes 786436
  14.2 17.8 %collective-permute-start.9 = (bf16[8,128,128]{2,1,0:T(8,128)(2,1)}, bf16[8,128,128]{2,1,0:T(8,128)(2,1)S(1)}, u32[]{:S(2)}, u32[]{:S(2)}) collective-permute-start(bf16[8,128,128]{2,1,0:T(8,128)(2,1)} %get-tuple-element.30), channel_id=1, source_target_pairs={{0,3},{1,2},{2,1},{3,0},{4,7},{5,6},{6,5},{7,4},{8,11},{9,10},{10,... | collective-permute-start | bytes 786440 | tf_op jit(solution)/shard_map/ppermute | solution.py:217
  21.2 15.5 %collective-permute-start.3 = (bf16[2,4,128,128]{3,2,1,0:T(8,128)(2,1)}, bf16[2,4,128,128]{3,2,1,0:T(8,128)(2,1)S(1)}, u32[]{:S(2)}, u32[]{:S(2)}) collective-permute-start(bf16[2,4,128,128]{3,2,1,0:T(8,128)(2,1)} %get-tuple-element.25), channel_id=1, source_target_pairs={{0,2},{1,3},{2,0},{3,1},{4,6},{5,7},{6,4},{7,5},{8,10},{9,11},{10,... | collective-permute-start | bytes 786440 | tf_op jit(solution)/shard_map/ppermute | solution.py:217
  22.4 39.4 %copy-start.4 = (bf16[8,128,128]{2,1,0:T(8,128)(2,1)}, bf16[8,128,128]{2,1,0:T(8,128)(2,1)S(1)}, u32[]{:S(2)}) copy-start(bf16[8,128,128]{2,1,0:T(8,128)(2,1)S(1)} %collective-permute-done.7.refs_9_) | copy-start | bytes 786436
  22.4 38.7 %collective-permute-start = (bf16[2,8,128,128]{3,2,1,0:T(8,128)(2,1)S(1)}, bf16[2,8,128,128]{3,2,1,0:T(8,128)(2,1)S(1)}, u32[]{:S(2)}, u32[]{:S(2)}) collective-permute-start(bf16[2,8,128,128]{3,2,1,0:T(8,128)(2,1)S(1)} %copy-done), channel_id=1, source_target_pairs={{0,4},{1,5},{2,6},{3,7},{4,8},{5,9},{6,10},{7,11},{8,12},{9,13},{1... | collective-permute-start | bytes 1572872 | tf_op jit(solution)/shard_map/ppermute | solution.py:217
  25.6 36.2 %copy-start.1 = (bf16[2,8,128,128]{3,2,1,0:T(8,128)(2,1)}, bf16[2,8,128,128]{3,2,1,0:T(8,128)(2,1)S(1)}, u32[]{:S(2)}) copy-start(bf16[2,8,128,128]{3,2,1,0:T(8,128)(2,1)S(1)} %collective-permute-done.1.refs_5_) | copy-start | bytes 1572868
  25.6 35.5 %collective-permute-start.2 = (bf16[2,8,128,128]{3,2,1,0:T(8,128)(2,1)S(1)}, bf16[2,8,128,128]{3,2,1,0:T(8,128)(2,1)S(1)}, u32[]{:S(2)}, u32[]{:S(2)}) collective-permute-start(bf16[2,8,128,128]{3,2,1,0:T(8,128)(2,1)S(1)} %collective-permute-done.1.refs_5_), channel_id=1, source_target_pairs={{0,4},{1,5},{2,6},{3,7},{4,8},{5,9},{6,10},{7,11},{8,12},{9,13},{1... | collective-permute-start | bytes 1572872 | tf_op jit(solution)/shard_map/ppermute | solution.py:217
  28.7 14.0 %collective-permute-start.5 = (bf16[2,4,128,128]{3,2,1,0:T(8,128)(2,1)}, bf16[2,4,128,128]{3,2,1,0:T(8,128)(2,1)}, u32[]{:S(2)}, u32[]{:S(2)}) collective-permute-start(bf16[2,4,128,128]{3,2,1,0:T(8,128)(2,1)} %get-tuple-element.26), channel_id=1, source_target_pairs={{0,3},{1,2},{2,1},{3,0},{4,7},{5,6},{6,5},{7,4},{8,11},{9,10},{10,... | collective-permute-start | bytes 786440 | tf_op jit(solution)/shard_map/ppermute | solution.py:217
  32.0 23.5 %collective-permute-start.11 = (bf16[2,4,128,128]{3,2,1,0:T(8,128)(2,1)S(1)}, bf16[2,4,128,128]{3,2,1,0:T(8,128)(2,1)S(1)}, u32[]{:S(2)}, u32[]{:S(2)}) collective-permute-start(bf16[2,4,128,128]{3,2,1,0:T(8,128)(2,1)S(1)} %collective-permute-done.10.refs_6_), channel_id=1, source_target_pairs={{0,4},{1,5},{2,6},{3,7},{4,8},{5,9},{6,10},{7,11},{8,12},{9,13},{1... | collective-permute-start | bytes 786440 | tf_op jit(solution)/shard_map/ppermute | solution.py:217
  36.7 36.0 %copy-start.8 = (bf16[2,4,128,128]{3,2,1,0:T(8,128)(2,1)}, bf16[2,4,128,128]{3,2,1,0:T(8,128)(2,1)S(1)}, u32[]{:S(2)}) copy-start(bf16[2,4,128,128]{3,2,1,0:T(8,128)(2,1)S(1)} %collective-permute-done.3.refs_6_) | copy-start | bytes 786436
  36.7 24.4 %collective-permute-start.13 = (bf16[2,4,128,128]{3,2,1,0:T(8,128)(2,1)}, bf16[2,4,128,128]{3,2,1,0:T(8,128)(2,1)S(1)}, u32[]{:S(2)}, u32[]{:S(2)}) collective-permute-start(bf16[2,4,128,128]{3,2,1,0:T(8,128)(2,1)} %copy-done.9), channel_id=1, source_target_pairs={{0,4},{1,5},{2,6},{3,7},{4,8},{5,9},{6,10},{7,11},{8,12},{9,13},{1... | collective-permute-start | bytes 786440 | tf_op jit(solution)/shard_map/ppermute | solution.py:217
  42.8 33.1 %collective-permute-start.4 = (bf16[2,4,128,128]{3,2,1,0:T(8,128)(2,1)S(1)}, bf16[2,4,128,128]{3,2,1,0:T(8,128)(2,1)}, u32[]{:S(2)}, u32[]{:S(2)}) collective-permute-start(bf16[2,4,128,128]{3,2,1,0:T(8,128)(2,1)S(1)} %collective-permute-done.3.refs_6_), channel_id=1, source_target_pairs={{0,4},{1,5},{2,6},{3,7},{4,8},{5,9},{6,10},{7,11},{8,12},{9,13},{1... | collective-permute-start | bytes 786440 | tf_op jit(solution)/shard_map/ppermute | solution.py:217
  55.5 20.4 %collective-permute-start.6 = (bf16[2,4,128,128]{3,2,1,0:T(8,128)(2,1)}, bf16[2,4,128,128]{3,2,1,0:T(8,128)(2,1)}, u32[]{:S(2)}, u32[]{:S(2)}) collective-permute-start(bf16[2,4,128,128]{3,2,1,0:T(8,128)(2,1)} %collective-permute-done.5.refs_7_), channel_id=1, source_target_pairs={{0,4},{1,5},{2,6},{3,7},{4,8},{5,9},{6,10},{7,11},{8,12},{9,13},{1... | collective-permute-start | bytes 786440 | tf_op jit(solution)/shard_map/ppermute | solution.py:217
  72.7 14.2 %collective-permute-start.15 = (bf16[4,128,128]{2,1,0:T(8,128)(2,1)}, bf16[4,128,128]{2,1,0:T(8,128)(2,1)S(1)}, u32[]{:S(2)}, u32[]{:S(2)}) collective-permute-start(bf16[4,128,128]{2,1,0:T(8,128)(2,1)} %get-tuple-element.36), channel_id=1, source_target_pairs={{0,1},{1,0},{2,3},{3,2},{4,5},{5,4},{6,7},{7,6},{8,9},{9,8},{10,11... | collective-permute-start | bytes 393224 | tf_op jit(solution)/shard_map/ppermute | solution.py:217
  74.2 14.5 %collective-permute-start.17 = (bf16[4,128,128]{2,1,0:T(8,128)(2,1)}, bf16[4,128,128]{2,1,0:T(8,128)(2,1)S(1)}, u32[]{:S(2)}, u32[]{:S(2)}) collective-permute-start(bf16[4,128,128]{2,1,0:T(8,128)(2,1)} %get-tuple-element.38), channel_id=1, source_target_pairs={{0,2},{1,3},{2,0},{3,1},{4,6},{5,7},{6,4},{7,5},{8,10},{9,11},{10,... | collective-permute-start | bytes 393224 | tf_op jit(solution)/shard_map/ppermute | solution.py:217
  74.5 14.2 %collective-permute-start.19 = (bf16[4,128,128]{2,1,0:T(8,128)(2,1)}, bf16[4,128,128]{2,1,0:T(8,128)(2,1)S(1)}, u32[]{:S(2)}, u32[]{:S(2)}) collective-permute-start(bf16[4,128,128]{2,1,0:T(8,128)(2,1)} %get-tuple-element.40), channel_id=1, source_target_pairs={{0,3},{1,2},{2,1},{3,0},{4,7},{5,6},{6,5},{7,4},{8,11},{9,10},{10,... | collective-permute-start | bytes 393224 | tf_op jit(solution)/shard_map/ppermute | solution.py:217
  86.4 2.2 %collective-permute-start.14 = (bf16[4,128,128]{2,1,0:T(8,128)(2,1)}, bf16[4,128,128]{2,1,0:T(8,128)(2,1)S(1)}, u32[]{:S(2)}, u32[]{:S(2)}) collective-permute-start(bf16[4,128,128]{2,1,0:T(8,128)(2,1)} %get-tuple-element.35), channel_id=1, source_target_pairs={{0,1},{1,0},{2,3},{3,2},{4,5},{5,4},{6,7},{7,6},{8,9},{9,8},{10,11... | collective-permute-start | bytes 393224 | tf_op jit(solution)/shard_map/ppermute | solution.py:217
  86.7 4.9 %collective-permute-start.16 = (bf16[4,128,128]{2,1,0:T(8,128)(2,1)}, bf16[4,128,128]{2,1,0:T(8,128)(2,1)S(1)}, u32[]{:S(2)}, u32[]{:S(2)}) collective-permute-start(bf16[4,128,128]{2,1,0:T(8,128)(2,1)} %get-tuple-element.37), channel_id=1, source_target_pairs={{0,2},{1,3},{2,0},{3,1},{4,6},{5,7},{6,4},{7,5},{8,10},{9,11},{10,... | collective-permute-start | bytes 393224 | tf_op jit(solution)/shard_map/ppermute | solution.py:217
  87.0 7.9 %collective-permute-start.18 = (bf16[4,128,128]{2,1,0:T(8,128)(2,1)}, bf16[4,128,128]{2,1,0:T(8,128)(2,1)S(1)}, u32[]{:S(2)}, u32[]{:S(2)}) collective-permute-start(bf16[4,128,128]{2,1,0:T(8,128)(2,1)} %get-tuple-element.39), channel_id=1, source_target_pairs={{0,3},{1,2},{2,1},{3,0},{4,7},{5,6},{6,5},{7,4},{8,11},{9,10},{10,... | collective-permute-start | bytes 393224 | tf_op jit(solution)/shard_map/ppermute | solution.py:217
  (15 other events, 118.3 us)
